TPU v7x, 32 devices: a whole 2x2x4 slice. The times are simulated.
32 devices in a mesh: ctx: 8 (over z, x), head: 4 (over y, core).
Axes of the slice: x: 2, y: 2, z: 4, core: 2. Of those that a mesh axis runs over, the one named last changes fastest.
Arguments:
- queries: bfloat16 [3072, 8192], P(('ctx', 'head')), may hold values from -6 to 6
- keys: bfloat16 [3072, 1024], P(('ctx', 'head')), may hold values from -6 to 6
- values: bfloat16 [3072, 1024], P(('ctx', 'head')), may hold values from -6 to 6
- attn_out: bfloat16 [3072, 8192], P('ctx', 'head'), may hold values from -6 to 6
- out_grad: bfloat16 [3072, 8192], P('ctx', 'head'), may hold values from -12 to 12
- log_sum: float32 [64, 3072], P('head', 'ctx'), as said below
- file_ids: int32 [3072], P('ctx'), may hold values from 0 to 7, as said below
Outputs:
- q_grad: bfloat16 [3072, 8192], P(('ctx', 'head'))
- k_grad: bfloat16 [3072, 1024], P(('ctx', 'head'))
- v_grad: bfloat16 [3072, 1024], P(('ctx', 'head'))
Inputs may be any that keep to these rules, and one draw needn't show every extreme that they name: file_ids never fall along the tokens, so each file's tokens are consecutive; each of the 8 files holds 1 to 1536 tokens, and the first file holds exactly 1536. log_sum is positive.
All inputs are finite; a program needn't handle non-finite values.
Results may differ from a plain program's by a relative error of at most 0.0053.
Values may be sent and summed in bfloat16 or wider, within the bound.
No kernel may reach another device: no remote copies, remote signals or barrier semaphores. Data moves between devices by JAX's collectives and lax.ppermute only.
A program may use at most 64 MiB of HBM per device.

v0:
```python
import math
import jax
import jax.numpy as jnp
from jax import lax
from jax.sharding import PartitionSpec as P

DH = 128


def passed_along(block, axis, distance):
    devices = range(lax.axis_size(axis))
    route = [(i - distance, i) for i in devices if i - distance in devices]
    return lax.ppermute(block, axis, route)


def shifted(block, axis, distance):
    devices = range(lax.axis_size(axis))
    route = [((i - distance) % len(devices), i) for i in devices]
    return lax.ppermute(block, axis, route)


def tile_grads(q_four, g_four, lse_three, delta_three, key_part, value_part, allowed):
    score_scale = 1.0 / math.sqrt(q_four.shape[-1])
    scores = (
        jnp.einsum("rkgd,ckd->kgrc", q_four, key_part, preferred_element_type=jnp.float32)
        * score_scale
    )
    attn_probs = jnp.exp(jnp.where(allowed[None, None], scores - lse_three[..., None], -1e30))
    probs_low = attn_probs.astype(jnp.bfloat16)
    dprobs = jnp.einsum("rkgd,ckd->kgrc", g_four, value_part, preferred_element_type=jnp.float32)
    dscores_low = (attn_probs * (dprobs - delta_three[..., None])).astype(jnp.bfloat16)
    q_part = jnp.einsum("kgrc,ckd->rkgd", dscores_low, key_part, preferred_element_type=jnp.float32)
    k_part = jnp.einsum("kgrc,rkgd->ckd", dscores_low, q_four, preferred_element_type=jnp.float32)
    v_part = jnp.einsum("kgrc,rkgd->ckd", probs_low, g_four, preferred_element_type=jnp.float32)
    return (q_part, k_part, v_part)


def per_device(queries, keys, values, attn_out, out_grad, log_sum, file_ids):
    q_rows, key_rows, value_rows = (
        lax.all_to_all(queries, "head", split_axis=1, concat_axis=0, tiled=True),
        lax.all_to_all(keys, "head", split_axis=1, concat_axis=0, tiled=True),
        lax.all_to_all(values, "head", split_axis=1, concat_axis=0, tiled=True),
    )
    block_rows = q_rows.shape[0]
    kv_local = key_rows.shape[1] // DH
    group_size = q_rows.shape[1] // (DH * kv_local)
    score_scale = 1.0 / math.sqrt(DH)
    q_four = q_rows.reshape(block_rows, kv_local, group_size, DH)
    g_four = out_grad.reshape(block_rows, kv_local, group_size, DH)
    o_four = attn_out.reshape(block_rows, kv_local, group_size, DH)
    key_three = key_rows.reshape(block_rows, kv_local, DH)
    value_three = value_rows.reshape(block_rows, kv_local, DH)
    lse_three = log_sum.reshape(kv_local, group_size, block_rows)
    delta_three = jnp.einsum("rkgd,rkgd->kgr", g_four, o_four, preferred_element_type=jnp.float32)
    ctx_count = lax.axis_size("ctx")
    reach_back = ctx_count // 2
    own_index = lax.axis_index("ctx")
    offsets = jnp.arange(block_rows, dtype=jnp.int32)
    query_pos = own_index * block_rows + offsets
    own_tags = file_ids.astype(jnp.bfloat16)
    grad_shape = (block_rows, kv_local, DH)

    def block_grads(key_part, value_part, tag_part, anchor):
        key_pos = anchor * block_rows + offsets
        allowed = (own_tags[:, None] == tag_part[None, :]) & (
            key_pos[None, :] <= query_pos[:, None]
        )

        def compute():
            return tile_grads(q_four, g_four, lse_three, delta_three, key_part, value_part, allowed)

        def skipped():
            return (
                jnp.zeros(q_four.shape, jnp.float32),
                jnp.zeros(grad_shape, jnp.float32),
                jnp.zeros(grad_shape, jnp.float32),
            )

        return lax.cond(jnp.any(allowed), compute, skipped)

    dq_first, dk_first, dv_first = block_grads(key_three, value_three, own_tags, own_index)
    k_store, v_store = (dk_first, dv_first)

    def visit_block(step_index, loop_state):
        dq_acc, key_part, value_part, tag_part, k_store, v_store = loop_state
        anchor = (own_index - step_index) % ctx_count
        key_part, value_part, tag_part = passed_along((key_part, value_part, tag_part), "ctx", 1)
        q_part, k_part, v_part = block_grads(key_part, value_part, tag_part, anchor)
        k_store, v_store = shifted((k_store, v_store), "ctx", 1)
        k_store = k_store + k_part
        v_store = v_store + v_part
        return (dq_acc + q_part, key_part, value_part, tag_part, k_store, v_store)

    loop_state = lax.fori_loop(
        1,
        reach_back + 1,
        visit_block,
        (dq_first, key_three, value_three, own_tags, k_store, v_store),
    )
    dq_sum = loop_state[0]
    k_total, v_total = shifted((loop_state[4], loop_state[5]), "ctx", -reach_back)
    q_done = (
        (dq_sum * score_scale).astype(jnp.bfloat16).reshape(block_rows, kv_local * group_size * DH)
    )
    k_done = (k_total * score_scale).astype(jnp.bfloat16).reshape(block_rows, kv_local * DH)
    v_done = v_total.astype(jnp.bfloat16).reshape(block_rows, kv_local * DH)
    q_grad, k_grad, v_grad = (
        lax.all_to_all(q_done, "head", split_axis=0, concat_axis=1, tiled=True),
        lax.all_to_all(k_done, "head", split_axis=0, concat_axis=1, tiled=True),
        lax.all_to_all(v_done, "head", split_axis=0, concat_axis=1, tiled=True),
    )
    return (q_grad, k_grad, v_grad)


def solution(mesh):
    return jax.shard_map(
        per_device,
        mesh=mesh,
        in_specs=(
            P(("ctx", "head"), None),
            P(("ctx", "head"), None),
            P(("ctx", "head"), None),
            P("ctx", "head"),
            P("ctx", "head"),
            P("head", "ctx"),
            P("ctx"),
        ),
        out_specs=(P(("ctx", "head"), None), P(("ctx", "head"), None), P(("ctx", "head"), None)),
        check_vma=False,
    )
```

profile of v0, /device:TPU:0, one launch (start us, length us, event | category | flops | bytes accessed | tf_op | source)
XLA Modules:
  0.0 267.3 jit_solution(12738604949703533861)
XLA Ops:
  2.4 4.2 %all-to-all-start = ((bf16[96,4,256]{2,0,1:T(8,128)(2,1)}), bf16[96,4,256]{2,0,1:T(8,128)(2,1)S(1)}, u32[]{:S(2)}, u32[]{:S(2)}) async-start(bf16[96,4,256]{2,0,1:T(8,128)(2,1)} %bitcast.126), calls=%async_computation | async-start | bytes 393216 | tf_op jit(solution)/shard_map/all_to_all | solution.py:41
  20.6 4.4 %all-to-all-start.1 = ((bf16[96,4,2048]{2,0,1:T(8,128)(2,1)}), bf16[96,4,2048]{2,0,1:T(8,128)(2,1)}, u32[]{:S(2)}, u32[]{:S(2)}) async-start(bf16[96,4,2048]{2,0,1:T(8,128)(2,1)} %bitcast.124), calls=%async_computation.1 | async-start | bytes 3145728 | tf_op jit(solution)/shard_map/all_to_all | solution.py:40
  41.0 4.2 %all-to-all-done.1 = bf16[96,4,2048]{2,0,1:T(8,128)(2,1)} async-done(((bf16[96,4,2048]{2,0,1:T(8,128)(2,1)}), bf16[96,4,2048]{2,0,1:T(8,128)(2,1)}, u32[]{:S(2)}, u32[]{:S(2)}) %all-to-all-start.1) | async-done | bytes 1572896 | tf_op jit(solution)/shard_map/all_to_all | solution.py:40
  48.5 10.1 %conditional.2 = (f32[384,2,8,128]{3,0,2,1:T(8,128)S(1)}, f32[384,2,128]{2,0,1:T(8,128)S(1)}, f32[384,2,128]{2,0,1:T(8,128)S(1)}) conditional(s32[]{:T(128)} %convert_element_type.38, () %tuple.46, (pred[384,384]{0,1:T(8,128)(4,1)}, bf16[384,2,128]{2,1,0:T(2,128)(2,1)S(1)}, bf16[384,2,8,128]{3,2,1,0:T(8,128)(2,1)S(1)}, f32[16,384]{1,0:T(8,128)}, ...), branch_computations={%region_1.0_spmd, %region_2.3_spmd} | conditional | flops 3043491840 | bytes 54337616 | solution.py:79
  60.5 145.0 %while.26 = (s32[]{:T(128)}, f32[384,2,8,128]{3,0,2,1:T(8,128)}, bf16[384,2,128]{2,0,1:T(8,128)(2,1)}, bf16[384,2,128]{2,0,1:T(8,128)(2,1)}, bf16[384]{0:T(512)(...) while((s32[]{:T(128)}, f32[384,2,8,128]{3,0,2,1:T(8,128)}, ...), condition=%wide.region_7.8_spmd.clone, body=%wide.region_3.7_spmd.clone.sunk | while | flops 3045360384 | bytes 84480736 | solution.py:94
  60.5 3.9 %collective-permute-start = (bf16[384]{0:T(512)(128)(2,1)S(1)}, bf16[384]{0:T(512)(128)(2,1)S(1)}, u32[]{:S(2)}, u32[]{:S(2)}) collective-permute-start(bf16[384]{0:T(512)(128)(2,1)S(1)} %get-tuple-element.651), channel_id=1, source_target_pairs={{0,4},{4,8},{8,12},{12,16},{16,20},{20,24},{24,28},{1,5},{5,9},{9,... | collective-permute-start | bytes 2312 | tf_op jit(solution)/shard_map/while/body/eval_jaxpr/ppermute | solution.py:13
  77.5 3.8 %add.135 = f32[384,2,8,128]{3,0,2,1:T(8,128)} add(f32[384,2,8,128]{3,0,2,1:T(8,128)} %get-tuple-element.648, f32[384,2,8,128]{3,0,2,1:T(8,128)S(1)} %get-tuple-element.613) | non-fusion elementwise | flops 786432 | bytes 9437184 | tf_op jit(solution)/shard_map/while/body/eval_jaxpr/add | solution.py:92
  82.7 3.8 %collective-permute-done.4 = f32[384,2,128]{2,0,1:T(8,128)} collective-permute-done((f32[384,2,128]{2,0,1:T(8,128)}, f32[384,2,128]{2,0,1:T(8,128)}, u32[]{:S(2)}, u32[]{:S(2)}) %collective-permute-start.4) | collective-permute-done | bytes 393248 | tf_op jit(solution)/shard_map/while/body/eval_jaxpr/ppermute | solution.py:19
  88.3 4.7 %collective-permute-done.3 = f32[384,2,128]{2,0,1:T(8,128)} collective-permute-done((f32[384,2,128]{2,0,1:T(8,128)}, f32[384,2,128]{2,0,1:T(8,128)}, u32[]{:S(2)}, u32[]{:S(2)}) %collective-permute-start.3) | collective-permute-done | bytes 393248 | tf_op jit(solution)/shard_map/while/body/eval_jaxpr/ppermute | solution.py:19
  94.8 6.9 %collective-permute-start = (bf16[384]{0:T(512)(128)(2,1)S(1)}, bf16[384]{0:T(512)(128)(2,1)S(1)}, u32[]{:S(2)}, u32[]{:S(2)}) collective-permute-start(bf16[384]{0:T(512)(128)(2,1)S(1)} %get-tuple-element.651), channel_id=1, source_target_pairs={{0,4},{4,8},{8,12},{12,16},{16,20},{20,24},{24,28},{1,5},{5,9},{9,... | collective-permute-start | bytes 2312 | tf_op jit(solution)/shard_map/while/body/eval_jaxpr/ppermute | solution.py:13
  101.7 4.3 %collective-permute-start.2 = (bf16[384,2,128]{2,0,1:T(8,128)(2,1)}, bf16[384,2,128]{2,0,1:T(8,128)(2,1)S(1)}, u32[]{:S(2)}, u32[]{:S(2)}) collective-permute-start(bf16[384,2,128]{2,0,1:T(8,128)(2,1)} %get-tuple-element.650), channel_id=1, source_target_pairs={{0,4},{4,8},{8,12},{12,16},{16,20},{20,24},{24,28},{1,5},{5,9},{9,... | collective-permute-start | bytes 589832 | tf_op jit(solution)/shard_map/while/body/eval_jaxpr/ppermute | solution.py:13
  116.1 3.8 %add.135 = f32[384,2,8,128]{3,0,2,1:T(8,128)} add(f32[384,2,8,128]{3,0,2,1:T(8,128)} %get-tuple-element.648, f32[384,2,8,128]{3,0,2,1:T(8,128)S(1)} %get-tuple-element.613) | non-fusion elementwise | flops 786432 | bytes 9437184 | tf_op jit(solution)/shard_map/while/body/eval_jaxpr/add | solution.py:92
  131.4 4.4 %collective-permute-start = (bf16[384]{0:T(512)(128)(2,1)S(1)}, bf16[384]{0:T(512)(128)(2,1)S(1)}, u32[]{:S(2)}, u32[]{:S(2)}) collective-permute-start(bf16[384]{0:T(512)(128)(2,1)S(1)} %get-tuple-element.651), channel_id=1, source_target_pairs={{0,4},{4,8},{8,12},{12,16},{16,20},{20,24},{24,28},{1,5},{5,9},{9,... | collective-permute-start | bytes 2312 | tf_op jit(solution)/shard_map/while/body/eval_jaxpr/ppermute | solution.py:13
  135.8 7.9 %collective-permute-start.2 = (bf16[384,2,128]{2,0,1:T(8,128)(2,1)}, bf16[384,2,128]{2,0,1:T(8,128)(2,1)S(1)}, u32[]{:S(2)}, u32[]{:S(2)}) collective-permute-start(bf16[384,2,128]{2,0,1:T(8,128)(2,1)} %get-tuple-element.650), channel_id=1, source_target_pairs={{0,4},{4,8},{8,12},{12,16},{16,20},{20,24},{24,28},{1,5},{5,9},{9,... | collective-permute-start | bytes 589832 | tf_op jit(solution)/shard_map/while/body/eval_jaxpr/ppermute | solution.py:13
  149.4 4.2 %collective-permute-done.1 = bf16[384,2,128]{2,0,1:T(8,128)(2,1)S(1)} collective-permute-done((bf16[384,2,128]{2,0,1:T(8,128)(2,1)}, bf16[384,2,128]{2,0,1:T(8,128)(2,1)S(1)}, u32[]{:S(2)}, u32[]{:S(2)}) %collective-permute-start.1) | collective-permute-done | bytes 196640 | tf_op jit(solution)/shard_map/while/body/eval_jaxpr/ppermute | solution.py:13
  154.0 3.8 %add.135 = f32[384,2,8,128]{3,0,2,1:T(8,128)} add(f32[384,2,8,128]{3,0,2,1:T(8,128)} %get-tuple-element.648, f32[384,2,8,128]{3,0,2,1:T(8,128)S(1)} %get-tuple-element.613) | non-fusion elementwise | flops 786432 | bytes 9437184 | tf_op jit(solution)/shard_map/while/body/eval_jaxpr/add | solution.py:92
  166.2 4.4 %collective-permute-start = (bf16[384]{0:T(512)(128)(2,1)S(1)}, bf16[384]{0:T(512)(128)(2,1)S(1)}, u32[]{:S(2)}, u32[]{:S(2)}) collective-permute-start(bf16[384]{0:T(512)(128)(2,1)S(1)} %get-tuple-element.651), channel_id=1, source_target_pairs={{0,4},{4,8},{8,12},{12,16},{16,20},{20,24},{24,28},{1,5},{5,9},{9,... | collective-permute-start | bytes 2312 | tf_op jit(solution)/shard_map/while/body/eval_jaxpr/ppermute | solution.py:13
  170.6 3.8 %collective-permute-start.2 = (bf16[384,2,128]{2,0,1:T(8,128)(2,1)}, bf16[384,2,128]{2,0,1:T(8,128)(2,1)S(1)}, u32[]{:S(2)}, u32[]{:S(2)}) collective-permute-start(bf16[384,2,128]{2,0,1:T(8,128)(2,1)} %get-tuple-element.650), channel_id=1, source_target_pairs={{0,4},{4,8},{8,12},{12,16},{16,20},{20,24},{24,28},{1,5},{5,9},{9,... | collective-permute-start | bytes 589832 | tf_op jit(solution)/shard_map/while/body/eval_jaxpr/ppermute | solution.py:13
  174.4 8.2 %collective-permute-start.1 = (bf16[384,2,128]{2,0,1:T(8,128)(2,1)}, bf16[384,2,128]{2,0,1:T(8,128)(2,1)S(1)}, u32[]{:S(2)}, u32[]{:S(2)}) collective-permute-start(bf16[384,2,128]{2,0,1:T(8,128)(2,1)} %get-tuple-element.649), channel_id=1, source_target_pairs={{0,4},{4,8},{8,12},{12,16},{16,20},{20,24},{24,28},{1,5},{5,9},{9,... | collective-permute-start | bytes 589832 | tf_op jit(solution)/shard_map/while/body/eval_jaxpr/ppermute | solution.py:13
  187.9 3.8 %add.135 = f32[384,2,8,128]{3,0,2,1:T(8,128)} add(f32[384,2,8,128]{3,0,2,1:T(8,128)} %get-tuple-element.648, f32[384,2,8,128]{3,0,2,1:T(8,128)S(1)} %get-tuple-element.613) | non-fusion elementwise | flops 786432 | bytes 9437184 | tf_op jit(solution)/shard_map/while/body/eval_jaxpr/add | solution.py:92
  197.1 6.6 %collective-permute-done.3 = f32[384,2,128]{2,0,1:T(8,128)} collective-permute-done((f32[384,2,128]{2,0,1:T(8,128)}, f32[384,2,128]{2,0,1:T(8,128)}, u32[]{:S(2)}, u32[]{:S(2)}) %collective-permute-start.3) | collective-permute-done | bytes 393248 | tf_op jit(solution)/shard_map/while/body/eval_jaxpr/ppermute | solution.py:19
  205.5 10.5 %collective-permute-start.5 = (f32[384,2,128]{2,0,1:T(8,128)}, f32[384,2,128]{2,0,1:T(8,128)}, u32[]{:S(2)}, u32[]{:S(2)}) collective-permute-start(f32[384,2,128]{2,0,1:T(8,128)} %get-tuple-element.410), channel_id=1, source_target_pairs={{16,0},{20,4},{24,8},{28,12},{0,16},{4,20},{8,24},{12,28},{17,1},{... | collective-permute-start | bytes 1179656 | tf_op jit(solution)/shard_map/ppermute | solution.py:19
  217.2 6.8 %collective-permute-done.6 = bf16[384,2,128]{2,0,1:T(8,128)(2,1)S(1)} collective-permute-done((bf16[384,2,128]{2,0,1:T(8,128)(2,1)S(1)}, bf16[384,2,128]{2,0,1:T(8,128)(2,1)S(1)}, u32[]{:S(2)}, u32[]{:S(2)}) %collective-permute-start.6) | collective-permute-done | bytes 196640 | tf_op jit(solution)/shard_map/ppermute | solution.py:19
  247.4 18.7 %all-to-all-done.3 = bf16[4,96,2048]{2,1,0:T(8,128)(2,1)S(1)} async-done(((bf16[4,96,2048]{2,1,0:T(8,128)(2,1)}), bf16[4,96,2048]{2,1,0:T(8,128)(2,1)S(1)}, u32[]{:S(2)}, u32[]{:S(2)}) %all-to-all-start.3) | async-done | bytes 1572896 | tf_op jit(solution)/shard_map/all_to_all | solution.py:108
  (144 shorter events, 136.8 us)
Async XLA Ops:
  2.4 9.6 %all-to-all-start = ((bf16[96,4,256]{2,0,1:T(8,128)(2,1)}), bf16[96,4,256]{2,0,1:T(8,128)(2,1)S(1)}, u32[]{:S(2)}, u32[]{:S(2)}) async-start(bf16[96,4,256]{2,0,1:T(8,128)(2,1)} %bitcast.126), calls=%async_computation | async-start | bytes 393216 | tf_op jit(solution)/shard_map/all_to_all | solution.py:41
  20.6 24.5 %all-to-all-start.1 = ((bf16[96,4,2048]{2,0,1:T(8,128)(2,1)}), bf16[96,4,2048]{2,0,1:T(8,128)(2,1)}, u32[]{:S(2)}, u32[]{:S(2)}) async-start(bf16[96,4,2048]{2,0,1:T(8,128)(2,1)} %bitcast.124), calls=%async_computation.1 | async-start | bytes 3145728 | tf_op jit(solution)/shard_map/all_to_all | solution.py:40
  60.5 13.9 %collective-permute-start = (bf16[384]{0:T(512)(128)(2,1)S(1)}, bf16[384]{0:T(512)(128)(2,1)S(1)}, u32[]{:S(2)}, u32[]{:S(2)}) collective-permute-start(bf16[384]{0:T(512)(128)(2,1)S(1)} %get-tuple-element.651), channel_id=1, source_target_pairs={{0,4},{4,8},{8,12},{12,16},{16,20},{20,24},{24,28},{1,5},{5,9},{9,... | collective-permute-start | bytes 2312 | tf_op jit(solution)/shard_map/while/body/eval_jaxpr/ppermute | solution.py:13
  64.5 12.2 %collective-permute-start.2 = (bf16[384,2,128]{2,0,1:T(8,128)(2,1)}, bf16[384,2,128]{2,0,1:T(8,128)(2,1)S(1)}, u32[]{:S(2)}, u32[]{:S(2)}) collective-permute-start(bf16[384,2,128]{2,0,1:T(8,128)(2,1)} %get-tuple-element.650), channel_id=1, source_target_pairs={{0,4},{4,8},{8,12},{12,16},{16,20},{20,24},{24,28},{1,5},{5,9},{9,... | collective-permute-start | bytes 589832 | tf_op jit(solution)/shard_map/while/body/eval_jaxpr/ppermute | solution.py:13
  68.0 9.2 %collective-permute-start.1 = (bf16[384,2,128]{2,0,1:T(8,128)(2,1)}, bf16[384,2,128]{2,0,1:T(8,128)(2,1)S(1)}, u32[]{:S(2)}, u32[]{:S(2)}) collective-permute-start(bf16[384,2,128]{2,0,1:T(8,128)(2,1)} %get-tuple-element.649), channel_id=1, source_target_pairs={{0,4},{4,8},{8,12},{12,16},{16,20},{20,24},{24,28},{1,5},{5,9},{9,... | collective-permute-start | bytes 589832 | tf_op jit(solution)/shard_map/while/body/eval_jaxpr/ppermute | solution.py:13
  71.4 15.1 %collective-permute-start.4 = (f32[384,2,128]{2,0,1:T(8,128)}, f32[384,2,128]{2,0,1:T(8,128)}, u32[]{:S(2)}, u32[]{:S(2)}) collective-permute-start(f32[384,2,128]{2,0,1:T(8,128)} %get-tuple-element.653), channel_id=1, source_target_pairs={{28,0},{0,4},{4,8},{8,12},{12,16},{16,20},{20,24},{24,28},{29,1},{... | collective-permute-start | bytes 1179656 | tf_op jit(solution)/shard_map/while/body/eval_jaxpr/ppermute | solution.py:19
  73.0 20.0 %collective-permute-start.3 = (f32[384,2,128]{2,0,1:T(8,128)}, f32[384,2,128]{2,0,1:T(8,128)}, u32[]{:S(2)}, u32[]{:S(2)}) collective-permute-start(f32[384,2,128]{2,0,1:T(8,128)} %get-tuple-element.652), channel_id=1, source_target_pairs={{28,0},{0,4},{4,8},{8,12},{12,16},{16,20},{20,24},{24,28},{29,1},{... | collective-permute-start | bytes 1179656 | tf_op jit(solution)/shard_map/while/body/eval_jaxpr/ppermute | solution.py:19
  94.8 16.9 %collective-permute-start = (bf16[384]{0:T(512)(128)(2,1)S(1)}, bf16[384]{0:T(512)(128)(2,1)S(1)}, u32[]{:S(2)}, u32[]{:S(2)}) collective-permute-start(bf16[384]{0:T(512)(128)(2,1)S(1)} %get-tuple-element.651), channel_id=1, source_target_pairs={{0,4},{4,8},{8,12},{12,16},{16,20},{20,24},{24,28},{1,5},{5,9},{9,... | collective-permute-start | bytes 2312 | tf_op jit(solution)/shard_map/while/body/eval_jaxpr/ppermute | solution.py:13
  101.7 12.2 %collective-permute-start.2 = (bf16[384,2,128]{2,0,1:T(8,128)(2,1)}, bf16[384,2,128]{2,0,1:T(8,128)(2,1)S(1)}, u32[]{:S(2)}, u32[]{:S(2)}) collective-permute-start(bf16[384,2,128]{2,0,1:T(8,128)(2,1)} %get-tuple-element.650), channel_id=1, source_target_pairs={{0,4},{4,8},{8,12},{12,16},{16,20},{20,24},{24,28},{1,5},{5,9},{9,... | collective-permute-start | bytes 589832 | tf_op jit(solution)/shard_map/while/body/eval_jaxpr/ppermute | solution.py:13
  105.9 9.8 %collective-permute-start.1 = (bf16[384,2,128]{2,0,1:T(8,128)(2,1)}, bf16[384,2,128]{2,0,1:T(8,128)(2,1)S(1)}, u32[]{:S(2)}, u32[]{:S(2)}) collective-permute-start(bf16[384,2,128]{2,0,1:T(8,128)(2,1)} %get-tuple-element.649), channel_id=1, source_target_pairs={{0,4},{4,8},{8,12},{12,16},{16,20},{20,24},{24,28},{1,5},{5,9},{9,... | collective-permute-start | bytes 589832 | tf_op jit(solution)/shard_map/while/body/eval_jaxpr/ppermute | solution.py:13
  108.6 15.5 %collective-permute-start.4 = (f32[384,2,128]{2,0,1:T(8,128)}, f32[384,2,128]{2,0,1:T(8,128)}, u32[]{:S(2)}, u32[]{:S(2)}) collective-permute-start(f32[384,2,128]{2,0,1:T(8,128)} %get-tuple-element.653), channel_id=1, source_target_pairs={{28,0},{0,4},{4,8},{8,12},{12,16},{16,20},{20,24},{24,28},{29,1},{... | collective-permute-start | bytes 1179656 | tf_op jit(solution)/shard_map/while/body/eval_jaxpr/ppermute | solution.py:19
  108.7 21.0 %collective-permute-start.3 = (f32[384,2,128]{2,0,1:T(8,128)}, f32[384,2,128]{2,0,1:T(8,128)}, u32[]{:S(2)}, u32[]{:S(2)}) collective-permute-start(f32[384,2,128]{2,0,1:T(8,128)} %get-tuple-element.652), channel_id=1, source_target_pairs={{28,0},{0,4},{4,8},{8,12},{12,16},{16,20},{20,24},{24,28},{29,1},{... | collective-permute-start | bytes 1179656 | tf_op jit(solution)/shard_map/while/body/eval_jaxpr/ppermute | solution.py:19
  131.4 15.0 %collective-permute-start = (bf16[384]{0:T(512)(128)(2,1)S(1)}, bf16[384]{0:T(512)(128)(2,1)S(1)}, u32[]{:S(2)}, u32[]{:S(2)}) collective-permute-start(bf16[384]{0:T(512)(128)(2,1)S(1)} %get-tuple-element.651), channel_id=1, source_target_pairs={{0,4},{4,8},{8,12},{12,16},{16,20},{20,24},{24,28},{1,5},{5,9},{9,... | collective-permute-start | bytes 2312 | tf_op jit(solution)/shard_map/while/body/eval_jaxpr/ppermute | solution.py:13
  135.8 13.6 %collective-permute-start.2 = (bf16[384,2,128]{2,0,1:T(8,128)(2,1)}, bf16[384,2,128]{2,0,1:T(8,128)(2,1)S(1)}, u32[]{:S(2)}, u32[]{:S(2)}) collective-permute-start(bf16[384,2,128]{2,0,1:T(8,128)(2,1)} %get-tuple-element.650), channel_id=1, source_target_pairs={{0,4},{4,8},{8,12},{12,16},{16,20},{20,24},{24,28},{1,5},{5,9},{9,... | collective-permute-start | bytes 589832 | tf_op jit(solution)/shard_map/while/body/eval_jaxpr/ppermute | solution.py:13
  143.7 9.9 %collective-permute-start.1 = (bf16[384,2,128]{2,0,1:T(8,128)(2,1)}, bf16[384,2,128]{2,0,1:T(8,128)(2,1)S(1)}, u32[]{:S(2)}, u32[]{:S(2)}) collective-permute-start(bf16[384,2,128]{2,0,1:T(8,128)(2,1)} %get-tuple-element.649), channel_id=1, source_target_pairs={{0,4},{4,8},{8,12},{12,16},{16,20},{20,24},{24,28},{1,5},{5,9},{9,... | collective-permute-start | bytes 589832 | tf_op jit(solution)/shard_map/while/body/eval_jaxpr/ppermute | solution.py:13
  146.3 13.9 %collective-permute-start.4 = (f32[384,2,128]{2,0,1:T(8,128)}, f32[384,2,128]{2,0,1:T(8,128)}, u32[]{:S(2)}, u32[]{:S(2)}) collective-permute-start(f32[384,2,128]{2,0,1:T(8,128)} %get-tuple-element.653), channel_id=1, source_target_pairs={{28,0},{0,4},{4,8},{8,12},{12,16},{16,20},{20,24},{24,28},{29,1},{... | collective-permute-start | bytes 1179656 | tf_op jit(solution)/shard_map/while/body/eval_jaxpr/ppermute | solution.py:19
  146.3 18.0 %collective-permute-start.3 = (f32[384,2,128]{2,0,1:T(8,128)}, f32[384,2,128]{2,0,1:T(8,128)}, u32[]{:S(2)}, u32[]{:S(2)}) collective-permute-start(f32[384,2,128]{2,0,1:T(8,128)} %get-tuple-element.652), channel_id=1, source_target_pairs={{28,0},{0,4},{4,8},{8,12},{12,16},{16,20},{20,24},{24,28},{29,1},{... | collective-permute-start | bytes 1179656 | tf_op jit(solution)/shard_map/while/body/eval_jaxpr/ppermute | solution.py:19
  166.2 16.6 %collective-permute-start = (bf16[384]{0:T(512)(128)(2,1)S(1)}, bf16[384]{0:T(512)(128)(2,1)S(1)}, u32[]{:S(2)}, u32[]{:S(2)}) collective-permute-start(bf16[384]{0:T(512)(128)(2,1)S(1)} %get-tuple-element.651), channel_id=1, source_target_pairs={{0,4},{4,8},{8,12},{12,16},{16,20},{20,24},{24,28},{1,5},{5,9},{9,... | collective-permute-start | bytes 2312 | tf_op jit(solution)/shard_map/while/body/eval_jaxpr/ppermute | solution.py:13
  170.6 14.4 %collective-permute-start.2 = (bf16[384,2,128]{2,0,1:T(8,128)(2,1)}, bf16[384,2,128]{2,0,1:T(8,128)(2,1)S(1)}, u32[]{:S(2)}, u32[]{:S(2)}) collective-permute-start(bf16[384,2,128]{2,0,1:T(8,128)(2,1)} %get-tuple-element.650), channel_id=1, source_target_pairs={{0,4},{4,8},{8,12},{12,16},{16,20},{20,24},{24,28},{1,5},{5,9},{9,... | collective-permute-start | bytes 589832 | tf_op jit(solution)/shard_map/while/body/eval_jaxpr/ppermute | solution.py:13
  174.4 13.2 %collective-permute-start.1 = (bf16[384,2,128]{2,0,1:T(8,128)(2,1)}, bf16[384,2,128]{2,0,1:T(8,128)(2,1)S(1)}, u32[]{:S(2)}, u32[]{:S(2)}) collective-permute-start(bf16[384,2,128]{2,0,1:T(8,128)(2,1)} %get-tuple-element.649), channel_id=1, source_target_pairs={{0,4},{4,8},{8,12},{12,16},{16,20},{20,24},{24,28},{1,5},{5,9},{9,... | collective-permute-start | bytes 589832 | tf_op jit(solution)/shard_map/while/body/eval_jaxpr/ppermute | solution.py:13
  182.6 12.7 %collective-permute-start.4 = (f32[384,2,128]{2,0,1:T(8,128)}, f32[384,2,128]{2,0,1:T(8,128)}, u32[]{:S(2)}, u32[]{:S(2)}) collective-permute-start(f32[384,2,128]{2,0,1:T(8,128)} %get-tuple-element.653), channel_id=1, source_target_pairs={{28,0},{0,4},{4,8},{8,12},{12,16},{16,20},{20,24},{24,28},{29,1},{... | collective-permute-start | bytes 1179656 | tf_op jit(solution)/shard_map/while/body/eval_jaxpr/ppermute | solution.py:19
  182.6 21.1 %collective-permute-start.3 = (f32[384,2,128]{2,0,1:T(8,128)}, f32[384,2,128]{2,0,1:T(8,128)}, u32[]{:S(2)}, u32[]{:S(2)}) collective-permute-start(f32[384,2,128]{2,0,1:T(8,128)} %get-tuple-element.652), channel_id=1, source_target_pairs={{28,0},{0,4},{4,8},{8,12},{12,16},{16,20},{20,24},{24,28},{29,1},{... | collective-permute-start | bytes 1179656 | tf_op jit(solution)/shard_map/while/body/eval_jaxpr/ppermute | solution.py:19
  205.5 22.9 %collective-permute-start.5 = (f32[384,2,128]{2,0,1:T(8,128)}, f32[384,2,128]{2,0,1:T(8,128)}, u32[]{:S(2)}, u32[]{:S(2)}) collective-permute-start(f32[384,2,128]{2,0,1:T(8,128)} %get-tuple-element.410), channel_id=1, source_target_pairs={{16,0},{20,4},{24,8},{28,12},{0,16},{4,20},{8,24},{12,28},{17,1},{... | collective-permute-start | bytes 1179656 | tf_op jit(solution)/shard_map/ppermute | solution.py:19
  242.4 23.6 %all-to-all-start.3 = ((bf16[4,96,2048]{2,1,0:T(8,128)(2,1)}), bf16[4,96,2048]{2,1,0:T(8,128)(2,1)S(1)}, u32[]{:S(2)}, u32[]{:S(2)}) async-start(bf16[4,96,2048]{2,1,0:T(8,128)(2,1)} %all_to_all.87), calls=%async_computation.3 | async-start | bytes 3145728 | tf_op jit(solution)/shard_map/all_to_all | solution.py:108
  (15 other events, 147.9 us)
where the time goes:
time: 269 us; the launch traced here: 267 us
  starting transfers between devices  95.2 us (35%)
  waiting for transfers between devices  78.2 us (29%)
  other arithmetic  42.8 us (16%)
  local copies, waits for them, and re-layouts  36.6 us (14%)
  matrix products  9.83 us (4%)
  loops' own time  3.25 us (1%)
    ppermute x12, starting transfers between devices, passed_along(): return lax.ppermute(block, axis, route)  55.8 us
    ppermute x10, waiting for transfers between devices, shifted(): return lax.ppermute(block, axis, route)  34.2 us
    all_to_all x1, waiting for transfers between devices, per_device(): lax.all_to_all(q_done, 'head', split_axis=0, concat_axis=1, tiled=True)  18.7 us
    ppermute x10, starting transfers between devices, shifted(): return lax.ppermute(block, axis, route)  17.1 us
    add x4, other arithmetic, visit_block(): return (dq_acc + q_part, key_part, value_part, tag_part, k_store, v_store)  15.4 us
    unnamed x27, local copies, waits for them, and re-layouts  13.2 us
    ppermute x12, waiting for transfers between devices, passed_along(): return lax.ppermute(block, axis, route)  9.85 us
    add x4, other arithmetic, visit_block(): v_store = v_store + v_part  7.14 us
  transfers between devices with their start and end apart: 28, of which 20 were waited for; matrix products, arithmetic and copies ran while one was open for 23% of the time, Pallas kernels for 0%

commit v1 on v0

--- a/solution.py
+++ b/solution.py
@@ -5,6 +5,22 @@
 from jax.sharding import PartitionSpec as P
 
 DH = 128
+
+
+def pairwise_exchange(x, axis, split, join):
+    ways, here = (lax.axis_size(axis), lax.axis_index(axis))
+    width = x.shape[split] // ways
+    shape = list(x.shape)
+    shape[split] = width
+    height = shape[join]
+    shape[join] = height * ways
+    full = jnp.zeros(shape, x.dtype)
+    for mask in range(ways):
+        part = lax.dynamic_slice_in_dim(x, (here ^ mask) * width, width, axis=split)
+        if mask:
+            part = lax.ppermute(part, axis, [(d, d ^ mask) for d in range(ways)])
+        full = lax.dynamic_update_slice_in_dim(full, part, (here ^ mask) * height, axis=join)
+    return full
 
 
 def passed_along(block, axis, distance):
@@ -107,7 +123,7 @@
     q_grad, k_grad, v_grad = (
         lax.all_to_all(q_done, "head", split_axis=0, concat_axis=1, tiled=True),
         lax.all_to_all(k_done, "head", split_axis=0, concat_axis=1, tiled=True),
-        lax.all_to_all(v_done, "head", split_axis=0, concat_axis=1, tiled=True),
+        pairwise_exchange(v_done, "head", 0, 1),
     )
     return (q_grad, k_grad, v_grad)
 

time: 269 us -> 256 us (0.952)
  starting transfers between devices: 95.2 us -> 86.8 us
  waiting for transfers between devices: 78.2 us -> 74.8 us
    all_to_all x1, waiting for transfers between devices: 18.7 us -> 0.01 us  [per_device(): lax.all_to_all(q_done, 'head', split_axis=0, concat_axis=1, tiled=True)]
    ppermute x0 -> x3, waiting for transfers between devices: none -> 11.5 us  [pairwise_exchange(): part = lax.ppermute(part, axis, [(d, d ^ mask) for d in range(ways)])]
    ppermute x10, waiting for transfers between devices: 34.2 us -> 43.5 us  [shifted(): return lax.ppermute(block, axis, route)]
    ppermute x10, starting transfers between devices: 17.1 us -> 9.86 us  [shifted(): return lax.ppermute(block, axis, route)]
    all_to_all x1 -> x0, starting transfers between devices: 3.37 us -> none  [per_device(): lax.all_to_all(v_done, 'head', split_axis=0, concat_axis=1, tiled=True)]
    all_to_all x1 -> x0, waiting for transfers between devices: 3.23 us -> none  [per_device(): lax.all_to_all(v_done, 'head', split_axis=0, concat_axis=1, tiled=True)]
    unnamed x27 -> x29, local copies, waits for them, and re-layouts: 13.2 us -> 13.2 us
  transfers between devices with their start and end apart: 28 -> 30, of which waited for: 20 -> 19; matrix products, arithmetic and copies ran while one was open for 23% -> 23% of each run, Pallas kernels for 0% -> 0%
where the time goes in v1:
time: 256 us; the launch traced here: 255 us
  starting transfers between devices  86.8 us (34%)
  waiting for transfers between devices  74.8 us (29%)
  other arithmetic  43.1 us (17%)
  local copies, waits for them, and re-layouts  35 us (14%)
  matrix products  9.84 us (4%)
  loops' own time  3.47 us (1%)
    ppermute x12, starting transfers between devices, passed_along(): return lax.ppermute(block, axis, route)  55.9 us
    ppermute x10, waiting for transfers between devices, shifted(): return lax.ppermute(block, axis, route)  43.5 us
    add x4, other arithmetic, visit_block(): return (dq_acc + q_part, key_part, value_part, tag_part, k_store, v_store)  15.4 us
    unnamed x29, local copies, waits for them, and re-layouts  13.2 us
    ppermute x3, waiting for transfers between devices, pairwise_exchange(): part = lax.ppermute(part, axis, [(d, d ^ mask) for d in range(ways)])  11.5 us
    ppermute x10, starting transfers between devices, shifted(): return lax.ppermute(block, axis, route)  9.86 us
    ppermute x12, waiting for transfers between devices, passed_along(): return lax.ppermute(block, axis, route)  9.4 us
    add x4, other arithmetic, visit_block(): v_store = v_store + v_part  7.19 us
  transfers between devices with their start and end apart: 30, of which 19 were waited for; matrix products, arithmetic and copies ran while one was open for 23% of the time, Pallas kernels for 0%

profile of v1, /device:TPU:0, one launch (start us, length us, event | category | flops | bytes accessed | tf_op | source)
XLA Modules:
  0.0 254.6 jit_solution(15108518999430798465)
XLA Ops:
  2.4 4.2 %all-to-all-start = ((bf16[96,4,256]{2,0,1:T(8,128)(2,1)}), bf16[96,4,256]{2,0,1:T(8,128)(2,1)S(1)}, u32[]{:S(2)}, u32[]{:S(2)}) async-start(bf16[96,4,256]{2,0,1:T(8,128)(2,1)} %bitcast.130), calls=%async_computation | async-start | bytes 393216 | tf_op jit(solution)/shard_map/all_to_all | solution.py:57
  20.6 4.4 %all-to-all-start.1 = ((bf16[96,4,2048]{2,0,1:T(8,128)(2,1)}), bf16[96,4,2048]{2,0,1:T(8,128)(2,1)}, u32[]{:S(2)}, u32[]{:S(2)}) async-start(bf16[96,4,2048]{2,0,1:T(8,128)(2,1)} %bitcast.128), calls=%async_computation.1 | async-start | bytes 3145728 | tf_op jit(solution)/shard_map/all_to_all | solution.py:56
  40.9 4.2 %all-to-all-done.1 = bf16[96,4,2048]{2,0,1:T(8,128)(2,1)} async-done(((bf16[96,4,2048]{2,0,1:T(8,128)(2,1)}), bf16[96,4,2048]{2,0,1:T(8,128)(2,1)}, u32[]{:S(2)}, u32[]{:S(2)}) %all-to-all-start.1) | async-done | bytes 1572896 | tf_op jit(solution)/shard_map/all_to_all | solution.py:56
  48.5 10.1 %conditional.2 = (f32[384,2,8,128]{3,0,2,1:T(8,128)S(1)}, f32[384,2,128]{2,0,1:T(8,128)S(1)}, f32[384,2,128]{2,0,1:T(8,128)S(1)}) conditional(s32[]{:T(128)} %convert_element_type.38, () %tuple.46, (pred[384,384]{0,1:T(8,128)(4,1)}, bf16[384,2,128]{2,1,0:T(2,128)(2,1)S(1)}, bf16[384,2,8,128]{3,2,1,0:T(8,128)(2,1)S(1)}, f32[16,384]{1,0:T(8,128)}, ...), branch_computations={%region_1.0_spmd, %region_2.3_spmd} | conditional | flops 3043491840 | bytes 54337616 | solution.py:95
  60.6 143.3 %while.26 = (s32[]{:T(128)}, f32[384,2,8,128]{3,0,2,1:T(8,128)}, bf16[384,2,128]{2,0,1:T(8,128)(2,1)}, bf16[384,2,128]{2,0,1:T(8,128)(2,1)}, bf16[384]{0:T(512)(...) while((s32[]{:T(128)}, f32[384,2,8,128]{3,0,2,1:T(8,128)}, ...), condition=%wide.region_7.8_spmd.clone, body=%wide.region_3.7_spmd.clone.sunk | while | flops 3045360384 | bytes 84480736 | solution.py:110
  60.6 3.9 %collective-permute-start = (bf16[384]{0:T(512)(128)(2,1)S(1)}, bf16[384]{0:T(512)(128)(2,1)S(1)}, u32[]{:S(2)}, u32[]{:S(2)}) collective-permute-start(bf16[384]{0:T(512)(128)(2,1)S(1)} %get-tuple-element.655), channel_id=1, source_target_pairs={{0,4},{4,8},{8,12},{12,16},{16,20},{20,24},{24,28},{1,5},{5,9},{9,... | collective-permute-start | bytes 2312 | tf_op jit(solution)/shard_map/while/body/eval_jaxpr/ppermute | solution.py:29
  77.6 3.9 %add.167 = f32[384,2,8,128]{3,0,2,1:T(8,128)} add(f32[384,2,8,128]{3,0,2,1:T(8,128)} %get-tuple-element.652, f32[384,2,8,128]{3,0,2,1:T(8,128)S(1)} %get-tuple-element.617) | non-fusion elementwise | flops 786432 | bytes 9437184 | tf_op jit(solution)/shard_map/while/body/eval_jaxpr/add | solution.py:108
  82.8 3.8 %collective-permute-done.4 = f32[384,2,128]{2,0,1:T(8,128)} collective-permute-done((f32[384,2,128]{2,0,1:T(8,128)}, f32[384,2,128]{2,0,1:T(8,128)}, u32[]{:S(2)}, u32[]{:S(2)}) %collective-permute-start.4) | collective-permute-done | bytes 393248 | tf_op jit(solution)/shard_map/while/body/eval_jaxpr/ppermute | solution.py:35
  88.3 4.7 %collective-permute-done.3 = f32[384,2,128]{2,0,1:T(8,128)} collective-permute-done((f32[384,2,128]{2,0,1:T(8,128)}, f32[384,2,128]{2,0,1:T(8,128)}, u32[]{:S(2)}, u32[]{:S(2)}) %collective-permute-start.3) | collective-permute-done | bytes 393248 | tf_op jit(solution)/shard_map/while/body/eval_jaxpr/ppermute | solution.py:35
  94.8 6.9 %collective-permute-start = (bf16[384]{0:T(512)(128)(2,1)S(1)}, bf16[384]{0:T(512)(128)(2,1)S(1)}, u32[]{:S(2)}, u32[]{:S(2)}) collective-permute-start(bf16[384]{0:T(512)(128)(2,1)S(1)} %get-tuple-element.655), channel_id=1, source_target_pairs={{0,4},{4,8},{8,12},{12,16},{16,20},{20,24},{24,28},{1,5},{5,9},{9,... | collective-permute-start | bytes 2312 | tf_op jit(solution)/shard_map/while/body/eval_jaxpr/ppermute | solution.py:29
  101.7 4.2 %collective-permute-start.2 = (bf16[384,2,128]{2,0,1:T(8,128)(2,1)}, bf16[384,2,128]{2,0,1:T(8,128)(2,1)S(1)}, u32[]{:S(2)}, u32[]{:S(2)}) collective-permute-start(bf16[384,2,128]{2,0,1:T(8,128)(2,1)} %get-tuple-element.654), channel_id=1, source_target_pairs={{0,4},{4,8},{8,12},{12,16},{16,20},{20,24},{24,28},{1,5},{5,9},{9,... | collective-permute-start | bytes 589832 | tf_op jit(solution)/shard_map/while/body/eval_jaxpr/ppermute | solution.py:29
  116.1 3.9 %add.167 = f32[384,2,8,128]{3,0,2,1:T(8,128)} add(f32[384,2,8,128]{3,0,2,1:T(8,128)} %get-tuple-element.652, f32[384,2,8,128]{3,0,2,1:T(8,128)S(1)} %get-tuple-element.617) | non-fusion elementwise | flops 786432 | bytes 9437184 | tf_op jit(solution)/shard_map/while/body/eval_jaxpr/add | solution.py:108
  131.5 4.4 %collective-permute-start = (bf16[384]{0:T(512)(128)(2,1)S(1)}, bf16[384]{0:T(512)(128)(2,1)S(1)}, u32[]{:S(2)}, u32[]{:S(2)}) collective-permute-start(bf16[384]{0:T(512)(128)(2,1)S(1)} %get-tuple-element.655), channel_id=1, source_target_pairs={{0,4},{4,8},{8,12},{12,16},{16,20},{20,24},{24,28},{1,5},{5,9},{9,... | collective-permute-start | bytes 2312 | tf_op jit(solution)/shard_map/while/body/eval_jaxpr/ppermute | solution.py:29
  135.9 7.9 %collective-permute-start.2 = (bf16[384,2,128]{2,0,1:T(8,128)(2,1)}, bf16[384,2,128]{2,0,1:T(8,128)(2,1)S(1)}, u32[]{:S(2)}, u32[]{:S(2)}) collective-permute-start(bf16[384,2,128]{2,0,1:T(8,128)(2,1)} %get-tuple-element.654), channel_id=1, source_target_pairs={{0,4},{4,8},{8,12},{12,16},{16,20},{20,24},{24,28},{1,5},{5,9},{9,... | collective-permute-start | bytes 589832 | tf_op jit(solution)/shard_map/while/body/eval_jaxpr/ppermute | solution.py:29
  149.4 4.2 %collective-permute-done.1 = bf16[384,2,128]{2,0,1:T(8,128)(2,1)S(1)} collective-permute-done((bf16[384,2,128]{2,0,1:T(8,128)(2,1)}, bf16[384,2,128]{2,0,1:T(8,128)(2,1)S(1)}, u32[]{:S(2)}, u32[]{:S(2)}) %collective-permute-start.1) | collective-permute-done | bytes 196640 | tf_op jit(solution)/shard_map/while/body/eval_jaxpr/ppermute | solution.py:29
  154.0 3.9 %add.167 = f32[384,2,8,128]{3,0,2,1:T(8,128)} add(f32[384,2,8,128]{3,0,2,1:T(8,128)} %get-tuple-element.652, f32[384,2,8,128]{3,0,2,1:T(8,128)S(1)} %get-tuple-element.617) | non-fusion elementwise | flops 786432 | bytes 9437184 | tf_op jit(solution)/shard_map/while/body/eval_jaxpr/add | solution.py:108
  166.2 4.4 %collective-permute-start = (bf16[384]{0:T(512)(128)(2,1)S(1)}, bf16[384]{0:T(512)(128)(2,1)S(1)}, u32[]{:S(2)}, u32[]{:S(2)}) collective-permute-start(bf16[384]{0:T(512)(128)(2,1)S(1)} %get-tuple-element.655), channel_id=1, source_target_pairs={{0,4},{4,8},{8,12},{12,16},{16,20},{20,24},{24,28},{1,5},{5,9},{9,... | collective-permute-start | bytes 2312 | tf_op jit(solution)/shard_map/while/body/eval_jaxpr/ppermute | solution.py:29
  170.6 3.8 %collective-permute-start.2 = (bf16[384,2,128]{2,0,1:T(8,128)(2,1)}, bf16[384,2,128]{2,0,1:T(8,128)(2,1)S(1)}, u32[]{:S(2)}, u32[]{:S(2)}) collective-permute-start(bf16[384,2,128]{2,0,1:T(8,128)(2,1)} %get-tuple-element.654), channel_id=1, source_target_pairs={{0,4},{4,8},{8,12},{12,16},{16,20},{20,24},{24,28},{1,5},{5,9},{9,... | collective-permute-start | bytes 589832 | tf_op jit(solution)/shard_map/while/body/eval_jaxpr/ppermute | solution.py:29
  174.4 8.2 %collective-permute-start.1 = (bf16[384,2,128]{2,0,1:T(8,128)(2,1)}, bf16[384,2,128]{2,0,1:T(8,128)(2,1)S(1)}, u32[]{:S(2)}, u32[]{:S(2)}) collective-permute-start(bf16[384,2,128]{2,0,1:T(8,128)(2,1)} %get-tuple-element.653), channel_id=1, source_target_pairs={{0,4},{4,8},{8,12},{12,16},{16,20},{20,24},{24,28},{1,5},{5,9},{9,... | collective-permute-start | bytes 589832 | tf_op jit(solution)/shard_map/while/body/eval_jaxpr/ppermute | solution.py:29
  188.0 3.9 %add.167 = f32[384,2,8,128]{3,0,2,1:T(8,128)} add(f32[384,2,8,128]{3,0,2,1:T(8,128)} %get-tuple-element.652, f32[384,2,8,128]{3,0,2,1:T(8,128)S(1)} %get-tuple-element.617) | non-fusion elementwise | flops 786432 | bytes 9437184 | tf_op jit(solution)/shard_map/while/body/eval_jaxpr/add | solution.py:108
  197.2 4.9 %collective-permute-done.3 = f32[384,2,128]{2,0,1:T(8,128)} collective-permute-done((f32[384,2,128]{2,0,1:T(8,128)}, f32[384,2,128]{2,0,1:T(8,128)}, u32[]{:S(2)}, u32[]{:S(2)}) %collective-permute-start.3) | collective-permute-done | bytes 393248 | tf_op jit(solution)/shard_map/while/body/eval_jaxpr/ppermute | solution.py:35
  207.2 9.8 %collective-permute-done.5 = f32[384,2,128]{2,0,1:T(8,128)S(1)} collective-permute-done((f32[384,2,128]{2,0,1:T(8,128)}, f32[384,2,128]{2,0,1:T(8,128)S(1)}, u32[]{:S(2)}, u32[]{:S(2)}) %collective-permute-start.5) | collective-permute-done | bytes 393248 | tf_op jit(solution)/shard_map/ppermute | solution.py:35
  230.6 8.2 %collective-permute-done.6 = bf16[384,2,128]{2,0,1:T(8,128)(2,1)S(1)} collective-permute-done((bf16[384,2,128]{2,0,1:T(8,128)(2,1)S(1)}, bf16[384,2,128]{2,0,1:T(8,128)(2,1)S(1)}, u32[]{:S(2)}, u32[]{:S(2)}) %collective-permute-start.6) | collective-permute-done | bytes 196640 | tf_op jit(solution)/shard_map/ppermute | solution.py:35
  241.1 11.5 %collective-permute-done.8 = bf16[96,256]{1,0:T(8,128)(2,1)S(1)} collective-permute-done((bf16[96,256]{1,0:T(8,128)(2,1)S(1)}, bf16[96,256]{1,0:T(8,128)(2,1)S(1)}, u32[]{:S(2)}, u32[]{:S(2)}) %collective-permute-start.8) | collective-permute-done | bytes 49184 | tf_op jit(solution)/shard_map/ppermute | solution.py:21
  (153 shorter events, 132.1 us)
Async XLA Ops:
  20.6 24.5 %all-to-all-start.1 = ((bf16[96,4,2048]{2,0,1:T(8,128)(2,1)}), bf16[96,4,2048]{2,0,1:T(8,128)(2,1)}, u32[]{:S(2)}, u32[]{:S(2)}) async-start(bf16[96,4,2048]{2,0,1:T(8,128)(2,1)} %bitcast.128), calls=%async_computation.1 | async-start | bytes 3145728 | tf_op jit(solution)/shard_map/all_to_all | solution.py:56
  60.6 13.9 %collective-permute-start = (bf16[384]{0:T(512)(128)(2,1)S(1)}, bf16[384]{0:T(512)(128)(2,1)S(1)}, u32[]{:S(2)}, u32[]{:S(2)}) collective-permute-start(bf16[384]{0:T(512)(128)(2,1)S(1)} %get-tuple-element.655), channel_id=1, source_target_pairs={{0,4},{4,8},{8,12},{12,16},{16,20},{20,24},{24,28},{1,5},{5,9},{9,... | collective-permute-start | bytes 2312 | tf_op jit(solution)/shard_map/while/body/eval_jaxpr/ppermute | solution.py:29
  64.5 12.3 %collective-permute-start.2 = (bf16[384,2,128]{2,0,1:T(8,128)(2,1)}, bf16[384,2,128]{2,0,1:T(8,128)(2,1)S(1)}, u32[]{:S(2)}, u32[]{:S(2)}) collective-permute-start(bf16[384,2,128]{2,0,1:T(8,128)(2,1)} %get-tuple-element.654), channel_id=1, source_target_pairs={{0,4},{4,8},{8,12},{12,16},{16,20},{20,24},{24,28},{1,5},{5,9},{9,... | collective-permute-start | bytes 589832 | tf_op jit(solution)/shard_map/while/body/eval_jaxpr/ppermute | solution.py:29
  71.4 15.1 %collective-permute-start.4 = (f32[384,2,128]{2,0,1:T(8,128)}, f32[384,2,128]{2,0,1:T(8,128)}, u32[]{:S(2)}, u32[]{:S(2)}) collective-permute-start(f32[384,2,128]{2,0,1:T(8,128)} %get-tuple-element.657), channel_id=1, source_target_pairs={{28,0},{0,4},{4,8},{8,12},{12,16},{16,20},{20,24},{24,28},{29,1},{... | collective-permute-start | bytes 1179656 | tf_op jit(solution)/shard_map/while/body/eval_jaxpr/ppermute | solution.py:35
  73.0 20.0 %collective-permute-start.3 = (f32[384,2,128]{2,0,1:T(8,128)}, f32[384,2,128]{2,0,1:T(8,128)}, u32[]{:S(2)}, u32[]{:S(2)}) collective-permute-start(f32[384,2,128]{2,0,1:T(8,128)} %get-tuple-element.656), channel_id=1, source_target_pairs={{28,0},{0,4},{4,8},{8,12},{12,16},{16,20},{20,24},{24,28},{29,1},{... | collective-permute-start | bytes 1179656 | tf_op jit(solution)/shard_map/while/body/eval_jaxpr/ppermute | solution.py:35
  94.8 16.9 %collective-permute-start = (bf16[384]{0:T(512)(128)(2,1)S(1)}, bf16[384]{0:T(512)(128)(2,1)S(1)}, u32[]{:S(2)}, u32[]{:S(2)}) collective-permute-start(bf16[384]{0:T(512)(128)(2,1)S(1)} %get-tuple-element.655), channel_id=1, source_target_pairs={{0,4},{4,8},{8,12},{12,16},{16,20},{20,24},{24,28},{1,5},{5,9},{9,... | collective-permute-start | bytes 2312 | tf_op jit(solution)/shard_map/while/body/eval_jaxpr/ppermute | solution.py:29
  101.7 12.3 %collective-permute-start.2 = (bf16[384,2,128]{2,0,1:T(8,128)(2,1)}, bf16[384,2,128]{2,0,1:T(8,128)(2,1)S(1)}, u32[]{:S(2)}, u32[]{:S(2)}) collective-permute-start(bf16[384,2,128]{2,0,1:T(8,128)(2,1)} %get-tuple-element.654), channel_id=1, source_target_pairs={{0,4},{4,8},{8,12},{12,16},{16,20},{20,24},{24,28},{1,5},{5,9},{9,... | collective-permute-start | bytes 589832 | tf_op jit(solution)/shard_map/while/body/eval_jaxpr/ppermute | solution.py:29
  106.0 9.8 %collective-permute-start.1 = (bf16[384,2,128]{2,0,1:T(8,128)(2,1)}, bf16[384,2,128]{2,0,1:T(8,128)(2,1)S(1)}, u32[]{:S(2)}, u32[]{:S(2)}) collective-permute-start(bf16[384,2,128]{2,0,1:T(8,128)(2,1)} %get-tuple-element.653), channel_id=1, source_target_pairs={{0,4},{4,8},{8,12},{12,16},{16,20},{20,24},{24,28},{1,5},{5,9},{9,... | collective-permute-start | bytes 589832 | tf_op jit(solution)/shard_map/while/body/eval_jaxpr/ppermute | solution.py:29
  108.6 15.5 %collective-permute-start.4 = (f32[384,2,128]{2,0,1:T(8,128)}, f32[384,2,128]{2,0,1:T(8,128)}, u32[]{:S(2)}, u32[]{:S(2)}) collective-permute-start(f32[384,2,128]{2,0,1:T(8,128)} %get-tuple-element.657), channel_id=1, source_target_pairs={{28,0},{0,4},{4,8},{8,12},{12,16},{16,20},{20,24},{24,28},{29,1},{... | collective-permute-start | bytes 1179656 | tf_op jit(solution)/shard_map/while/body/eval_jaxpr/ppermute | solution.py:35
  108.7 21.0 %collective-permute-start.3 = (f32[384,2,128]{2,0,1:T(8,128)}, f32[384,2,128]{2,0,1:T(8,128)}, u32[]{:S(2)}, u32[]{:S(2)}) collective-permute-start(f32[384,2,128]{2,0,1:T(8,128)} %get-tuple-element.656), channel_id=1, source_target_pairs={{28,0},{0,4},{4,8},{8,12},{12,16},{16,20},{20,24},{24,28},{29,1},{... | collective-permute-start | bytes 1179656 | tf_op jit(solution)/shard_map/while/body/eval_jaxpr/ppermute | solution.py:35
  131.5 15.1 %collective-permute-start = (bf16[384]{0:T(512)(128)(2,1)S(1)}, bf16[384]{0:T(512)(128)(2,1)S(1)}, u32[]{:S(2)}, u32[]{:S(2)}) collective-permute-start(bf16[384]{0:T(512)(128)(2,1)S(1)} %get-tuple-element.655), channel_id=1, source_target_pairs={{0,4},{4,8},{8,12},{12,16},{16,20},{20,24},{24,28},{1,5},{5,9},{9,... | collective-permute-start | bytes 2312 | tf_op jit(solution)/shard_map/while/body/eval_jaxpr/ppermute | solution.py:29
  135.9 13.6 %collective-permute-start.2 = (bf16[384,2,128]{2,0,1:T(8,128)(2,1)}, bf16[384,2,128]{2,0,1:T(8,128)(2,1)S(1)}, u32[]{:S(2)}, u32[]{:S(2)}) collective-permute-start(bf16[384,2,128]{2,0,1:T(8,128)(2,1)} %get-tuple-element.654), channel_id=1, source_target_pairs={{0,4},{4,8},{8,12},{12,16},{16,20},{20,24},{24,28},{1,5},{5,9},{9,... | collective-permute-start | bytes 589832 | tf_op jit(solution)/shard_map/while/body/eval_jaxpr/ppermute | solution.py:29
  143.8 9.9 %collective-permute-start.1 = (bf16[384,2,128]{2,0,1:T(8,128)(2,1)}, bf16[384,2,128]{2,0,1:T(8,128)(2,1)S(1)}, u32[]{:S(2)}, u32[]{:S(2)}) collective-permute-start(bf16[384,2,128]{2,0,1:T(8,128)(2,1)} %get-tuple-element.653), channel_id=1, source_target_pairs={{0,4},{4,8},{8,12},{12,16},{16,20},{20,24},{24,28},{1,5},{5,9},{9,... | collective-permute-start | bytes 589832 | tf_op jit(solution)/shard_map/while/body/eval_jaxpr/ppermute | solution.py:29
  146.3 13.9 %collective-permute-start.4 = (f32[384,2,128]{2,0,1:T(8,128)}, f32[384,2,128]{2,0,1:T(8,128)}, u32[]{:S(2)}, u32[]{:S(2)}) collective-permute-start(f32[384,2,128]{2,0,1:T(8,128)} %get-tuple-element.657), channel_id=1, source_target_pairs={{28,0},{0,4},{4,8},{8,12},{12,16},{16,20},{20,24},{24,28},{29,1},{... | collective-permute-start | bytes 1179656 | tf_op jit(solution)/shard_map/while/body/eval_jaxpr/ppermute | solution.py:35
  146.4 18.1 %collective-permute-start.3 = (f32[384,2,128]{2,0,1:T(8,128)}, f32[384,2,128]{2,0,1:T(8,128)}, u32[]{:S(2)}, u32[]{:S(2)}) collective-permute-start(f32[384,2,128]{2,0,1:T(8,128)} %get-tuple-element.656), channel_id=1, source_target_pairs={{28,0},{0,4},{4,8},{8,12},{12,16},{16,20},{20,24},{24,28},{29,1},{... | collective-permute-start | bytes 1179656 | tf_op jit(solution)/shard_map/while/body/eval_jaxpr/ppermute | solution.py:35
  166.2 16.6 %collective-permute-start = (bf16[384]{0:T(512)(128)(2,1)S(1)}, bf16[384]{0:T(512)(128)(2,1)S(1)}, u32[]{:S(2)}, u32[]{:S(2)}) collective-permute-start(bf16[384]{0:T(512)(128)(2,1)S(1)} %get-tuple-element.655), channel_id=1, source_target_pairs={{0,4},{4,8},{8,12},{12,16},{16,20},{20,24},{24,28},{1,5},{5,9},{9,... | collective-permute-start | bytes 2312 | tf_op jit(solution)/shard_map/while/body/eval_jaxpr/ppermute | solution.py:29
  170.6 14.5 %collective-permute-start.2 = (bf16[384,2,128]{2,0,1:T(8,128)(2,1)}, bf16[384,2,128]{2,0,1:T(8,128)(2,1)S(1)}, u32[]{:S(2)}, u32[]{:S(2)}) collective-permute-start(bf16[384,2,128]{2,0,1:T(8,128)(2,1)} %get-tuple-element.654), channel_id=1, source_target_pairs={{0,4},{4,8},{8,12},{12,16},{16,20},{20,24},{24,28},{1,5},{5,9},{9,... | collective-permute-start | bytes 589832 | tf_op jit(solution)/shard_map/while/body/eval_jaxpr/ppermute | solution.py:29
  174.4 13.2 %collective-permute-start.1 = (bf16[384,2,128]{2,0,1:T(8,128)(2,1)}, bf16[384,2,128]{2,0,1:T(8,128)(2,1)S(1)}, u32[]{:S(2)}, u32[]{:S(2)}) collective-permute-start(bf16[384,2,128]{2,0,1:T(8,128)(2,1)} %get-tuple-element.653), channel_id=1, source_target_pairs={{0,4},{4,8},{8,12},{12,16},{16,20},{20,24},{24,28},{1,5},{5,9},{9,... | collective-permute-start | bytes 589832 | tf_op jit(solution)/shard_map/while/body/eval_jaxpr/ppermute | solution.py:29
  182.7 12.7 %collective-permute-start.4 = (f32[384,2,128]{2,0,1:T(8,128)}, f32[384,2,128]{2,0,1:T(8,128)}, u32[]{:S(2)}, u32[]{:S(2)}) collective-permute-start(f32[384,2,128]{2,0,1:T(8,128)} %get-tuple-element.657), channel_id=1, source_target_pairs={{28,0},{0,4},{4,8},{8,12},{12,16},{16,20},{20,24},{24,28},{29,1},{... | collective-permute-start | bytes 1179656 | tf_op jit(solution)/shard_map/while/body/eval_jaxpr/ppermute | solution.py:35
  182.7 19.3 %collective-permute-start.3 = (f32[384,2,128]{2,0,1:T(8,128)}, f32[384,2,128]{2,0,1:T(8,128)}, u32[]{:S(2)}, u32[]{:S(2)}) collective-permute-start(f32[384,2,128]{2,0,1:T(8,128)} %get-tuple-element.656), channel_id=1, source_target_pairs={{28,0},{0,4},{4,8},{8,12},{12,16},{16,20},{20,24},{24,28},{29,1},{... | collective-permute-start | bytes 1179656 | tf_op jit(solution)/shard_map/while/body/eval_jaxpr/ppermute | solution.py:35
  203.8 13.2 %collective-permute-start.5 = (f32[384,2,128]{2,0,1:T(8,128)}, f32[384,2,128]{2,0,1:T(8,128)S(1)}, u32[]{:S(2)}, u32[]{:S(2)}) collective-permute-start(f32[384,2,128]{2,0,1:T(8,128)} %get-tuple-element.410), channel_id=1, source_target_pairs={{16,0},{20,4},{24,8},{28,12},{0,16},{4,20},{8,24},{12,28},{17,1},{... | collective-permute-start | bytes 1179656 | tf_op jit(solution)/shard_map/ppermute | solution.py:35
  226.8 26.5 %all-to-all-start.3 = ((bf16[4,96,2048]{2,1,0:T(8,128)(2,1)}), bf16[4,96,2048]{2,1,0:T(8,128)(2,1)S(1)}, u32[]{:S(2)}, u32[]{:S(2)}) async-start(bf16[4,96,2048]{2,1,0:T(8,128)(2,1)} %all_to_all.73), calls=%async_computation.3 | async-start | bytes 3145728 | tf_op jit(solution)/shard_map/all_to_all | solution.py:124
  239.0 13.6 %collective-permute-start.9 = (bf16[96,256]{1,0:T(8,128)(2,1)S(1)}, bf16[96,256]{1,0:T(8,128)(2,1)S(1)}, u32[]{:S(2)}, u32[]{:S(2)}) collective-permute-start(bf16[96,256]{1,0:T(8,128)(2,1)S(1)} %get-tuple-element.519), channel_id=1, source_target_pairs={{0,3},{1,2},{2,1},{3,0},{4,7},{5,6},{6,5},{7,4},{8,11},{9,10},{10,... | collective-permute-start | bytes 147464 | tf_op jit(solution)/shard_map/ppermute | solution.py:21
  240.7 11.8 %collective-permute-start.8 = (bf16[96,256]{1,0:T(8,128)(2,1)S(1)}, bf16[96,256]{1,0:T(8,128)(2,1)S(1)}, u32[]{:S(2)}, u32[]{:S(2)}) collective-permute-start(bf16[96,256]{1,0:T(8,128)(2,1)S(1)} %get-tuple-element.520), channel_id=1, source_target_pairs={{0,2},{1,3},{2,0},{3,1},{4,6},{5,7},{6,4},{7,5},{8,10},{9,11},{10,... | collective-permute-start | bytes 147464 | tf_op jit(solution)/shard_map/ppermute | solution.py:21
  (18 other events, 138.6 us)
